TPU v7x, 32 devices: a whole 2x2x4 slice. The times are simulated.
32 devices in a mesh: vx: 4 (over y, x), vy: 8 (over z, core).
Axes of the slice: x: 2, y: 2, z: 4, core: 2. Of those that a mesh axis runs over, the one named last changes fastest.
Arguments:
- hidden: bfloat16 [128, 5120], P(('vx', 'vy')), may hold values from -96 to 96
- unembed: bfloat16 [152064, 5120], P(('vx', 'vy')), may hold values from -2 to 2
- loss_mask: int32 [128], P(('vx', 'vy')), may hold values 0 or 1
- seq_ids: int32 [128], P(('vx', 'vy')), may hold values from 0 to 7, never falling along the last dimension, each value on 1 to 32 neighbouring positions
Outputs:
- entropy: float32 [128], P(('vx', 'vy'))
- seq_mean: float32 [8], replicated
Inputs may be any that keep to these rules, and one draw needn't show every extreme that they name: `seq_ids`: sequence numbers never fall along the tokens; each sequence has 1 to 32 tokens.
All inputs are finite; a program needn't handle non-finite values. No bound on the sum of `loss_mask` on one device may be relied on, other than what follows from the above.
Results may differ from a plain program's by a relative error of at most 0.0013.
Values may be sent and summed in bfloat16 or wider, within the bound.
A program may use at most 128 MiB of HBM per device.

v0:
```python
import jax
import jax.numpy as jnp
from jax import lax
from jax.sharding import PartitionSpec as P

SEQS = 8


def sequence_sums(entropy_rows, mask_rows, id_rows):
    member = (id_rows[:, None] == jnp.arange(SEQS, dtype=jnp.int32)[None, :]) & (
        mask_rows[:, None] > 0
    )
    partial_sums = jnp.sum(entropy_rows[:, None] * member.astype(jnp.float32), axis=0)
    partial_counts = jnp.sum(member.astype(jnp.int32), axis=0)
    return (partial_sums, partial_counts)


def per_device(hidden, unembed, loss_mask, seq_ids):
    tok_local = hidden.shape[0]
    all_mask, all_ids = (
        lax.all_gather(loss_mask, ("vx", "vy"), axis=0, tiled=True),
        lax.all_gather(seq_ids, ("vx", "vy"), axis=0, tiled=True),
    )
    logits = lax.dot_general(
        unembed,
        lax.all_gather(hidden, ("vx", "vy"), axis=0, tiled=True),
        (((1,), (1,)), ((), ())),
        preferred_element_type=jnp.float32,
    )
    peaked = jnp.max(logits, axis=0)
    shifted = logits - peaked[None, :]
    expval = jnp.exp(shifted)
    stats = jnp.stack([peaked, jnp.sum(expval, axis=0), jnp.sum(expval * shifted, axis=0)])
    peaked, totals, tilted = (stats[0], stats[1], stats[2])
    position = lax.axis_index(("vx", "vy")) * tok_local
    largest = lax.pmax(peaked, ("vx", "vy"))
    shift = peaked - largest
    factor = jnp.exp(shift)
    norms_all, tilts_all = lax.psum(
        (factor * totals, factor * (tilted + shift * totals)), ("vx", "vy")
    )
    entropy_all = jnp.log(norms_all) - tilts_all / norms_all
    entropy = lax.dynamic_slice_in_dim(entropy_all, position, tok_local)
    seq_sums, seq_counts = sequence_sums(entropy_all, all_mask, all_ids)
    seq_mean = seq_sums / jnp.maximum(seq_counts, 1).astype(jnp.float32)
    return (entropy, seq_mean)


def solution(mesh):
    in_specs = (P(("vx", "vy"), None), P(("vx", "vy"), None), P(("vx", "vy")), P(("vx", "vy")))
    out_specs = (P(("vx", "vy")), P())
    return jax.shard_map(
        per_device, mesh=mesh, in_specs=in_specs, out_specs=out_specs, check_vma=False
    )
```

profile of v0, /device:TPU:0, one launch (start us, length us, event | category | flops | bytes accessed | tf_op | source)
XLA Modules:
  0.0 179.5 jit_solution(8160077383454973072)
XLA Ops:
  7.2 0.0 all-gather.3.cloned.1.call-start
  7.2 0.7 all-gather.3.cloned.1.call-update
  7.9 0.9 dynamic-update-slice
  8.8 0.8 dynamic-update-slice.1
  9.6 42.0 %all-reduce.2 = (s32[128]{0:T(128)S(1)}, s32[128]{0:T(128)S(1)}) all-reduce(s32[128]{0:T(128)S(1)} %dynamic-update-slice, s32[128]{0:T(128)S(1)} %dynamic-update-slice.1), channel_id=1, replica_groups=mesh['vx'=4,'vy'=8] {'vx','vy'}, use_global_device_ids=true, to_apply=%add | all-reduce | flops 256 | bytes 2048
  51.6 0.1 convert_reduce_fusion
  51.7 16.3 %all-gather.3.cloned.1.call-done = bf16[32,4,5120]{2,1,0:T(4,128)(2,1)} async-done(((bf16[1,4,5120]{2,1,0:T(4,128)(2,1)}), bf16[32,4,5120]{2,1,0:T(4,128)(2,1)}) %all-gather.3.cloned.1.call-update) | async-done | bytes 1310736 | tf_op jit(solution)/shard_map/all_gather | solution.py:26
  68.0 3.3 %reshape.14 = bf16[128,5120]{1,0:T(8,128)(2,1)} reshape(bf16[32,4,5120]{2,1,0:T(4,128)(2,1)} %all-gather.3.cloned.1.call-done) | data formatting | bytes 2621440
  71.3 20.4 %fusion.2 = (f32[128]{0:T(128)S(1)}, f32[4752,128]{1,0:T(8,128)S(1)}) fusion(bf16[4752,5120]{1,0:T(8,128)(2,1)} %param.5, bf16[128,5120]{1,0:T(8,128)(2,1)} %reshape.14), kind=kOutput, calls=%fused_computation.12 | convolution fusion | flops 6229149696 | bytes 52404736 | tf_op jit(solution)/shard_map/dot_general | solution.py:24
  91.7 39.1 %pmax.7 = f32[128]{0:T(128)S(1)} all-reduce(f32[128]{0:T(128)S(1)} %get-tuple-element.10), channel_id=1, replica_groups=mesh['vx'=4,'vy'=8] {'vx','vy'}, use_global_device_ids=true, to_apply=%region_1.0 | all-reduce | flops 128 | bytes 1024 | tf_op jit(solution)/shard_map/pmax | solution.py:36
  130.9 0.7 exponential_reduce_fusion
  131.5 39.9 %all-reduce.3 = (f32[128]{0:T(128)S(1)}, f32[128]{0:T(128)S(1)}) all-reduce(f32[128]{0:T(128)S(1)} %get-tuple-element.9, f32[128]{0:T(128)S(1)} %get-tuple-element.8), channel_id=1, replica_groups=mesh['vx'=4,'vy'=8] {'vx','vy'}, use_global_device_ids=true, to_apply=%region_5.0 | all-reduce | flops 256 | bytes 2048 | tf_op jit(solution)/shard_map/psum | solution.py:39
  171.5 0.1 select_reduce_fusion
  171.6 0.6 dynamic_slice.3
  172.2 0.5 convert_divide_fusion
  (5 shorter events, 0.0 us)
Async XLA Ops:
  7.2 60.9 %all-gather.3.cloned.1.call-start = ((), (), s32[]{:S(2)}) async-start(), calls=%async_computation | async-start | bytes 1351680 | tf_op jit(solution)/shard_map/all_gather | solution.py:26
Sparse Core Ops, SparseCore 0:
  10.8 57.1 all-gather.2
where the time goes:
time: 180 us
  blocking collectives  121 us (67%)
  matrix products  20.4 us (11%)
  waiting for transfers between devices  17 us (9%)
  between operations  14.1 us (8%)
  local copies, waits for them, and re-layouts  5.59 us (3%)
    unnamed x1, blocking collectives  42 us
    psum x1, blocking collectives, per_device(): lax.psum((factor * totals, factor * (tilted + shift * totals)), ('vx', 'v...  39.9 us
    pmax x1, blocking collectives, per_device(): largest = lax.pmax(peaked, ('vx', 'vy'))  39.1 us
    dot_general x1, matrix products, per_device(): lax.dot_general(unembed, lax.all_gather(hidden, ('vx', 'vy'), axis=0, til...  20.4 us
    all_gather x1, waiting for transfers between devices, per_device(): lax.all_gather(hidden, ('vx', 'vy'), axis=0, tiled=True)  16.3 us
    unnamed x5, local copies, waits for them, and re-layouts  5 us
  transfers between devices with their start and end apart: 1, of which 1 were waited for; matrix products, arithmetic and copies ran while one was open for 1% of the time, Pallas kernels for 0%

commit v1 on v0

--- a/solution.py
+++ b/solution.py
@@ -1,9 +1,18 @@
+import functools
 import jax
 import jax.numpy as jnp
 from jax import lax
 from jax.sharding import PartitionSpec as P
 
 SEQS = 8
+
+
+def _cut_series(q_in, a_name, axis_tag):
+    placed = lax.psum(q_in, a_name)
+    return lax.psum(placed, axis_tag)
+
+
+end_rows = functools.partial(_cut_series, a_name="vx", axis_tag="vy")
 
 
 def sequence_sums(entropy_rows, mask_rows, id_rows):
@@ -36,9 +45,7 @@
     largest = lax.pmax(peaked, ("vx", "vy"))
     shift = peaked - largest
     factor = jnp.exp(shift)
-    norms_all, tilts_all = lax.psum(
-        (factor * totals, factor * (tilted + shift * totals)), ("vx", "vy")
-    )
+    norms_all, tilts_all = end_rows((factor * totals, factor * (tilted + shift * totals)))
     entropy_all = jnp.log(norms_all) - tilts_all / norms_all
     entropy = lax.dynamic_slice_in_dim(entropy_all, position, tok_local)
     seq_sums, seq_counts = sequence_sums(entropy_all, all_mask, all_ids)

time: 180 us -> 164 us (0.911)
  blocking collectives: 121 us -> 105 us
    psum x1 -> x2, blocking collectives: 39.9 us -> 23.4 us  [the longest x1 13.6 us: _cut_series(): return lax.psum(placed, axis_tag)]
where the time goes in v1:
time: 164 us; the launch traced here: 163 us
  blocking collectives  105 us (64%)
  matrix products  20.4 us (12%)
  waiting for transfers between devices  17 us (10%)
  between operations  14.1 us (9%)
  local copies, waits for them, and re-layouts  5.59 us (3%)
    unnamed x1, blocking collectives  42 us
    pmax x1, blocking collectives, per_device(): largest = lax.pmax(peaked, ('vx', 'vy'))  39.2 us
    dot_general x1, matrix products, per_device(): lax.dot_general(unembed, lax.all_gather(hidden, ('vx', 'vy'), axis=0, til...  20.4 us
    all_gather x1, waiting for transfers between devices, per_device(): lax.all_gather(hidden, ('vx', 'vy'), axis=0, tiled=True)  16.3 us
    psum x1, blocking collectives, _cut_series(): return lax.psum(placed, axis_tag)  13.6 us
    psum x1, blocking collectives, _cut_series(): placed = lax.psum(q_in, a_name)  9.8 us
    unnamed x5, local copies, waits for them, and re-layouts  5 us
  transfers between devices with their start and end apart: 1, of which 1 were waited for; matrix products, arithmetic and copies ran while one was open for 1% of the time, Pallas kernels for 0%

profile of v1, /device:TPU:0, one launch (start us, length us, event | category | flops | bytes accessed | tf_op | source)
XLA Modules:
  0.0 163.0 jit_solution(6698702954244121656)
XLA Ops:
  7.2 0.0 all-gather.3.cloned.1.call-start
  7.2 0.7 all-gather.3.cloned.1.call-update
  7.9 0.9 dynamic-update-slice
  8.8 0.8 dynamic-update-slice.1
  9.6 42.0 %all-reduce.2 = (s32[128]{0:T(128)S(1)}, s32[128]{0:T(128)S(1)}) all-reduce(s32[128]{0:T(128)S(1)} %dynamic-update-slice, s32[128]{0:T(128)S(1)} %dynamic-update-slice.1), channel_id=1, replica_groups=mesh['vx'=4,'vy'=8] {'vx','vy'}, use_global_device_ids=true, to_apply=%add | all-reduce | flops 256 | bytes 2048
  51.6 0.1 convert_reduce_fusion
  51.7 16.3 %all-gather.3.cloned.1.call-done = bf16[32,4,5120]{2,1,0:T(4,128)(2,1)} async-done(((bf16[1,4,5120]{2,1,0:T(4,128)(2,1)}), bf16[32,4,5120]{2,1,0:T(4,128)(2,1)}) %all-gather.3.cloned.1.call-update) | async-done | bytes 1310736 | tf_op jit(solution)/shard_map/all_gather | solution.py:35
  68.0 3.3 %reshape.14 = bf16[128,5120]{1,0:T(8,128)(2,1)} reshape(bf16[32,4,5120]{2,1,0:T(4,128)(2,1)} %all-gather.3.cloned.1.call-done) | data formatting | bytes 2621440
  71.3 20.4 %fusion.2 = (f32[128]{0:T(128)S(1)}, f32[4752,128]{1,0:T(8,128)S(1)}) fusion(bf16[4752,5120]{1,0:T(8,128)(2,1)} %param.5, bf16[128,5120]{1,0:T(8,128)(2,1)} %reshape.14), kind=kOutput, calls=%fused_computation.12 | convolution fusion | flops 6229149696 | bytes 52404736 | tf_op jit(solution)/shard_map/dot_general | solution.py:33
  91.7 39.2 %pmax.7 = f32[128]{0:T(128)S(1)} all-reduce(f32[128]{0:T(128)S(1)} %get-tuple-element.12), channel_id=1, replica_groups=mesh['vx'=4,'vy'=8] {'vx','vy'}, use_global_device_ids=true, to_apply=%region_1.0 | all-reduce | flops 128 | bytes 1024 | tf_op jit(solution)/shard_map/pmax | solution.py:45
  130.9 0.7 exponential_reduce_fusion
  131.6 9.8 %all-reduce.4 = (f32[128]{0:T(128)S(1)}, f32[128]{0:T(128)S(1)}) all-reduce(f32[128]{0:T(128)S(1)} %get-tuple-element.11, f32[128]{0:T(128)S(1)} %get-tuple-element.10), channel_id=1, replica_groups=mesh['vx'=4,'vy'=8] {'vx'}, use_global_device_ids=true, to_apply=%region_6.0 | all-reduce | flops 256 | bytes 2048 | tf_op jit(solution)/shard_map/psum | solution.py:11
  141.4 13.6 %all-reduce.3 = (f32[128]{0:T(128)S(1)}, f32[128]{0:T(128)S(1)}) all-reduce(f32[128]{0:T(128)S(1)} %get-tuple-element.8, f32[128]{0:T(128)S(1)} %get-tuple-element.9), channel_id=1, replica_groups=mesh['vx'=4,'vy'=8] {'vy'}, use_global_device_ids=true, to_apply=%region_7.0 | all-reduce | flops 256 | bytes 2048 | tf_op jit(solution)/shard_map/psum | solution.py:12
  154.9 0.1 select_reduce_fusion
  155.1 0.6 dynamic_slice.3
  155.6 0.5 convert_divide_fusion
  (5 shorter events, 0.0 us)
Async XLA Ops:
  7.2 60.9 %all-gather.3.cloned.1.call-start = ((), (), s32[]{:S(2)}) async-start(), calls=%async_computation | async-start | bytes 1351680 | tf_op jit(solution)/shard_map/all_gather | solution.py:35
Sparse Core Ops, SparseCore 0:
  10.8 57.1 all-gather.2
